TPU v7x, 32 devices: a whole 2x2x4 slice. The times are simulated.
32 devices in a mesh: seq: 8 (over z, core), expert: 4 (over y, x).
Axes of the slice: x: 2, y: 2, z: 4, core: 2. Of those that a mesh axis runs over, the one named last changes fastest.
Arguments:
- tokens: bfloat16 [4, 32, 4096], P('expert', 'seq'), may hold values from -6 to 6
- out_grad: bfloat16 [4, 32, 4096], P('expert', 'seq'), may hold values from -12 to 12
- expert_ids: int32 [4, 32, 8], P('expert', 'seq'), may hold values from 0 to 15, as said below
- route_gates: bfloat16 [4, 32, 8], P('expert', 'seq'), may hold values from 0.019897461 to 0.5
- gate_weight: bfloat16 [16, 1536, 4096], P('expert', 'seq'), may hold values from -0.09375 to 0.09375
- up_weight: bfloat16 [16, 1536, 4096], P('expert', 'seq'), may hold values from -0.09375 to 0.09375
- down_weight: bfloat16 [16, 1536, 4096], P('expert', 'seq'), may hold values from -0.15625 to 0.15625
Outputs:
- token_grad: bfloat16 [4, 32, 4096], P('expert', 'seq')
Inputs may be any that keep to these rules, and one draw needn't show every extreme that they name: `expert_ids`: each token names 8 different experts; within each index of the first dimension (one group of 32 tokens) every expert is named at most 32 times, and some expert exactly 32 times.
All inputs are finite; a program needn't handle non-finite values.
Results may differ from a plain program's by a relative error of at most 0.0057.
Values may be sent and summed in bfloat16 or wider, within the bound.
No kernel may reach another device: no remote copies, remote signals or barrier semaphores. Data moves between devices by JAX's collectives and lax.ppermute only.
A program may use at most 128 MiB of HBM per device.

v0:
```python
import jax
import jax.numpy as jnp
from jax import lax
from jax.sharding import PartitionSpec as P


def swiglu_back(gate_act, up_act, hidden_grad):
    sigmoid = jax.nn.sigmoid(gate_act)
    d_gate = (hidden_grad * up_act * sigmoid * (1.0 + gate_act * (1.0 - sigmoid))).astype(
        jnp.bfloat16
    )
    d_up = (hidden_grad * gate_act * sigmoid).astype(jnp.bfloat16)
    return (d_gate, d_up)


def expert_grads(input_rows, grad_rows, gate_rows, gate_mat, up_mat, down_mat):
    gate_act = jnp.einsum("ird,ifd->ifr", input_rows, gate_mat, preferred_element_type=jnp.float32)
    up_act = jnp.einsum("ird,ifd->ifr", input_rows, up_mat, preferred_element_type=jnp.float32)
    down_back = jnp.einsum("ird,ifd->ifr", grad_rows, down_mat, preferred_element_type=jnp.float32)
    hidden_grad = down_back * gate_rows.astype(jnp.float32)[:, None, :]
    d_gate, d_up = swiglu_back(gate_act, up_act, hidden_grad)
    summed = jnp.einsum("ifr,ifd->ird", d_gate, gate_mat, preferred_element_type=jnp.float32)
    summed = summed + jnp.einsum("ifr,ifd->ird", d_up, up_mat, preferred_element_type=jnp.float32)
    return summed.astype(jnp.bfloat16)


def per_device(tokens, out_grad, expert_ids, route_gates, gate_weight, up_weight, down_weight):
    gathered_x, gathered_dy, gathered_ids, gathered_gates = (
        lax.all_gather(tokens, "seq", axis=1, tiled=True),
        lax.all_gather(out_grad, "seq", axis=1, tiled=True),
        lax.all_gather(expert_ids, "seq", axis=1, tiled=True),
        lax.all_gather(route_gates, "seq", axis=1, tiled=True),
    )
    group_x = gathered_x[0]
    group_dy = gathered_dy[0]
    group_idx = gathered_ids[0]
    group_gates = gathered_gates[0]
    group_size, top_count = group_idx.shape
    model_width = group_x.shape[1]
    local_experts = gate_weight.shape[0]
    expert_peers = lax.axis_size("expert")
    seq_size = lax.axis_size("seq")
    experts = local_experts * expert_peers
    capacity = 2 * group_size * top_count // experts
    flat_ids = group_idx.reshape(-1)
    onehot = (flat_ids[:, None] == jnp.arange(experts, dtype=jnp.int32)[None, :]).astype(jnp.int32)
    position = jnp.sum(jnp.cumsum(onehot, axis=0) * onehot, axis=1) - 1
    slot_index = flat_ids * capacity + position
    route_token = jnp.arange(flat_ids.shape[0], dtype=jnp.int32) // top_count
    slot_token = (
        jnp.full((experts * capacity,), group_size, jnp.int32).at[slot_index].set(route_token)
    )
    slot_gate = (
        jnp.zeros((experts * capacity,), jnp.bfloat16).at[slot_index].set(group_gates.reshape(-1))
    )
    slot_owner = slot_token
    slot_token = slot_token.reshape(expert_peers, local_experts, capacity)
    slot_gate = slot_gate.reshape(expert_peers, local_experts, capacity)
    padded_x = jnp.concatenate([group_x, jnp.zeros((1, model_width), jnp.bfloat16)], axis=0)
    padded_dy = jnp.concatenate([group_dy, jnp.zeros((1, model_width), jnp.bfloat16)], axis=0)
    share_len = capacity // seq_size
    start_slot = lax.axis_index("seq") * share_len
    part_token = lax.dynamic_slice_in_dim(slot_token, start_slot, share_len, 2)
    part_gate = lax.dynamic_slice_in_dim(slot_gate, start_slot, share_len, 2)
    send_x = jnp.take(padded_x, part_token, axis=0)
    send_dy = jnp.take(padded_dy, part_token, axis=0)
    arrived_x, arrived_dy, arrived_gate = (
        lax.all_to_all(send_x, "expert", split_axis=0, concat_axis=2, tiled=True),
        lax.all_to_all(send_dy, "expert", split_axis=0, concat_axis=2, tiled=True),
        lax.all_to_all(part_gate, "expert", split_axis=0, concat_axis=2, tiled=True),
    )
    recv_x, recv_dy, recv_gate = (
        lax.all_gather(arrived_x, "seq", axis=2, tiled=True),
        lax.all_gather(arrived_dy, "seq", axis=2, tiled=True),
        lax.all_gather(arrived_gate, "seq", axis=2, tiled=True),
    )
    part_rows = expert_grads(
        recv_x[0], recv_dy[0], recv_gate[0], gate_weight, up_weight, down_weight
    )
    reshaped = part_rows.reshape(
        local_experts, seq_size, expert_peers, capacity // seq_size, model_width
    )
    returned = lax.all_to_all(reshaped, "expert", split_axis=2, concat_axis=0, tiled=True)
    flat_parts = returned.reshape(experts * capacity, model_width)
    wanted = jnp.arange(lax.axis_size("seq") * tokens.shape[1], dtype=jnp.int32)
    selector = (wanted[:, None] == slot_owner[None, :]).astype(jnp.bfloat16)
    summed = lax.psum_scatter(
        jnp.dot(selector, flat_parts, preferred_element_type=jnp.float32),
        "seq",
        scatter_dimension=0,
        tiled=True,
    )
    return summed.astype(jnp.bfloat16)[None]


def solution(mesh):
    in_specs = (
        P("expert", "seq", None),
        P("expert", "seq", None),
        P("expert", "seq", None),
        P("expert", "seq", None),
        P("expert", "seq", None),
        P("expert", "seq", None),
        P("expert", "seq", None),
    )
    out_specs = P("expert", "seq", None)
    return jax.shard_map(
        per_device, mesh=mesh, in_specs=in_specs, out_specs=out_specs, check_vma=False
    )
```

profile of v0, /device:TPU:0, one launch (start us, length us, event | category | flops | bytes accessed | tf_op | source)
XLA Modules:
  0.0 310.6 jit_solution(13137008721957007697)
XLA Ops:
  6.5 14.7 %all_gather.21 = s32[1,32,8]{2,0,1:T(1,128)S(1)} all-gather(s32[1,4,8]{2,0,1:T(1,128)} %bitcast.102), channel_id=1, replica_groups=mesh['seq'=8,'expert'=4] {'seq'}, dimensions={1}, use_global_device_ids=true | all-gather | bytes 1152 | tf_op jit(solution)/shard_map/all_gather | solution.py:31
  21.4 0.6 reduce-window.6
  22.7 0.7 fusion.50
  23.7 1.4 scatter_custom_fusion
  25.4 0.8 copy.33
  26.2 14.9 %all_gather.22 = bf16[1,32,4096]{2,0,1:T(2,128)(2,1)S(1)} all-gather(bf16[1,4,4096]{2,0,1:T(2,128)(2,1)S(1)} %copy.33), channel_id=1, replica_groups=mesh['seq'=8,'expert'=4] {'seq'}, dimensions={1}, use_global_device_ids=true | all-gather | bytes 294912 | tf_op jit(solution)/shard_map/all_gather | solution.py:30
  41.4 0.9 gather_fusion
  42.6 14.7 %all_gather.26 = bf16[1,32,4096]{2,0,1:T(2,128)(2,1)S(1)} all-gather(bf16[1,4,4096]{2,0,1:T(2,128)(2,1)S(1)} %copy.39), channel_id=1, replica_groups=mesh['seq'=8,'expert'=4] {'seq'}, dimensions={1}, use_global_device_ids=true | all-gather | bytes 294912 | tf_op jit(solution)/shard_map/all_gather | solution.py:29
  57.6 0.9 gather_fusion.1
  58.7 0.6 broadcast_select_fusion
  59.3 12.5 %all_to_all.69 = bf16[4,4,4,4096]{3,2,1,0:T(4,128)(2,1)S(1)} all-to-all(bf16[4,4,4,4096]{3,2,1,0:T(4,128)(2,1)S(1)} %get-tuple-element.10), channel_id=1, replica_groups=mesh['seq'=8,'expert'=4] {'expert'}, dimensions={0} | all-to-all | bytes 1048576 | tf_op jit(solution)/shard_map/all_to_all | solution.py:68
  72.0 0.9 all_to_all.61
  73.0 10.2 %all_to_all.70 = bf16[4,4,4,4096]{3,2,1,0:T(4,128)(2,1)S(1)} all-to-all(bf16[4,4,4,4096]{3,2,1,0:T(4,128)(2,1)S(1)} %get-tuple-element.11), channel_id=1, replica_groups=mesh['seq'=8,'expert'=4] {'expert'}, dimensions={0} | all-to-all | bytes 1048576 | tf_op jit(solution)/shard_map/all_to_all | solution.py:69
  83.4 0.9 all_to_all.53
  84.4 13.4 %all_gather.24 = bf16[1,32,8]{2,0,1:T(2,128)(2,1)S(1)} all-gather(bf16[1,4,8]{2,0,1:T(2,128)(2,1)S(1)} %copy.35), channel_id=1, replica_groups=mesh['seq'=8,'expert'=4] {'seq'}, dimensions={1}, use_global_device_ids=true | all-gather | bytes 576 | tf_op jit(solution)/shard_map/all_gather | solution.py:32
  98.0 2.2 scatter_custom_fusion.1
  100.3 7.0 %all_to_all.71 = bf16[4,4,4]{2,1,0:T(4,128)(2,1)S(1)} all-to-all(bf16[4,4,4]{2,1,0:T(4,128)(2,1)S(1)} %constant_dynamic-slice_fusion), channel_id=1, replica_groups=mesh['seq'=8,'expert'=4] {'expert'}, dimensions={0} | all-to-all | bytes 256 | tf_op jit(solution)/shard_map/all_to_all | solution.py:70
  107.5 14.3 %all_gather.25 = bf16[1,4,128]{1,0,2:T(2,128)(2,1)S(1)} all-gather(bf16[1,4,16]{1,0,2:T(2,128)(2,1)S(1)} %reshape.126), channel_id=1, replica_groups=mesh['seq'=8,'expert'=4] {'seq'}, dimensions={2}, use_global_device_ids=true | all-gather | bytes 1152 | tf_op jit(solution)/shard_map/all_gather | solution.py:75
  121.9 5.9 %fusion.9 = f32[4,192,128]{2,1,0:T(8,128)S(1)} fusion(bf16[4,192,4096]{2,1,0:T(8,128)(2,1)} %param.13, bf16[1,4,128,4096]{3,2,1,0:T(8,128)(2,1)} %all-gather.5.cloned.1.call-done), kind=kOutput, calls=%fused_computation.12 | convolution fusion | flops 805306368 | bytes 10878976 | tf_op jit(solution)/shard_map/ird,ifd->ifr/dot_general | solution.py:17
  127.9 38.2 %all-gather.3.cloned.1.call-done = bf16[1,4,128,4096]{3,2,1,0:T(8,128)(2,1)} async-done(((bf16[1,4,16,4096]{3,2,1,0:T(8,128)(2,1)}), bf16[1,4,128,4096]{3,2,1,0:T(8,128)(2,1)}) %all-gather.3.cloned.1.call-update) | async-done | bytes 4194320 | tf_op jit(solution)/shard_map/all_gather | solution.py:74
  166.1 5.8 %fusion.24 = f32[4,192,128]{2,1,0:T(8,128)S(1)} fusion(bf16[4,192,4096]{2,1,0:T(8,128)(2,1)} %param.15, bf16[1,4,128,4096]{3,2,1,0:T(8,128)(2,1)} %all-gather.3.cloned.1.call-done, f32[4,128]{1,0:T(4,128)S(1)} %copy.38), kind=kOutput, calls=%fused_computation.17 | convolution fusion | flops 805404672 | bytes 10881024 | tf_op jit(solution)/shard_map/ird,ifd->ifr/dot_general | solution.py:19
  171.9 11.9 %fusion.31 = f32[4,128,4096]{2,1,0:T(8,128)} fusion(bf16[4,192,4096]{2,1,0:T(8,128)(2,1)} %param.13, f32[4,192,128]{2,1,0:T(8,128)S(1)} %fusion.24, bf16[4,192,4096]{2,1,0:T(8,128)(2,1)} %param.14, bf16[1,4,128,4096]{3,2,1,0:T(8,128)(2,1)} %all-gather.5.cloned.1.call-done, f32[4,192,128]{2,1,0:T(8,128)S(1)} %fusion.9), kind=kOutput, calls=%fused_computation.19 | convolution fusion | flops 1611595776 | bytes 25952256 | tf_op jit(solution)/shard_map/ifr,ifd->ird/dot_general | solution.py:22
  183.8 8.5 %add_convert_fusion = bf16[4,128,4096]{2,1,0:T(8,128)(2,1)} fusion(f32[4,128,4096]{2,1,0:T(8,128)} %fusion.31, bf16[4,192,4096]{2,1,0:T(8,128)(2,1)} %param.14, f32[4,192,128]{2,1,0:T(8,128)S(1)} %fusion.24, f32[4,192,128]{2,1,0:T(8,128)S(1)} %fusion.9), kind=kOutput, calls=%fused_computation.4 | convolution fusion | flops 810090496 | bytes 19660800 | tf_op jit(solution)/shard_map/ifr,ifd->ird/dot_general | solution.py:23
  192.4 7.2 %reshape.79 = bf16[4,8,4,4,4096]{4,3,2,1,0:T(4,128)(2,1)} reshape(bf16[4,128,4096]{2,1,0:T(8,128)(2,1)} %add_convert_fusion) | data formatting | bytes 8388608 | tf_op jit(solution)/shard_map/reshape | solution.py:80
  199.6 7.9 %copy.41 = bf16[4,8,4,4,4096]{4,3,1,0,2:T(4,128)(2,1)} copy(bf16[4,8,4,4,4096]{4,3,2,1,0:T(4,128)(2,1)} %reshape.79) | data formatting | bytes 8388608 | tf_op jit(solution)/shard_map/reshape | solution.py:80
  207.4 5.0 %all-to-all-start.3 = ((bf16[4,8,4,4,4096]{4,3,1,0,2:T(4,128)(2,1)}), bf16[4,8,4,4,4096]{4,3,1,0,2:T(4,128)(2,1)}, u32[]{:S(2)}, u32[]{:S(2)}) async-start(bf16[4,8,4,4,4096]{4,3,1,0,2:T(4,128)(2,1)} %copy.41), calls=%async_computation.3 | async-start | bytes 8388608 | tf_op jit(solution)/shard_map/all_to_all | solution.py:83
  212.5 0.6 dynamic-slice
  213.7 46.8 %all-to-all-done.3 = bf16[4,8,4,4,4096]{4,3,1,0,2:T(4,128)(2,1)} async-done(((bf16[4,8,4,4,4096]{4,3,1,0,2:T(4,128)(2,1)}), bf16[4,8,4,4,4096]{4,3,1,0,2:T(4,128)(2,1)}, u32[]{:S(2)}, u32[]{:S(2)}) %all-to-all-start.3) | async-done | bytes 4194336 | tf_op jit(solution)/shard_map/all_to_all | solution.py:83
  260.5 6.9 %reshape.80 = bf16[512,4096]{1,0:T(8,128)(2,1)} reshape(bf16[4,4,8,1,4,4096]{5,4,2,1,0,3:T(4,128)(2,1)} %bitcast.17) | data formatting | bytes 8388608 | tf_op jit(solution)/shard_map/reshape | solution.py:84
  267.4 3.0 fusion.38
  270.4 32.7 %all-reduce.4 = bf16[32,4096]{1,0:T(8,128)(2,1)S(1)} all-reduce(f32[32,4096]{1,0:T(8,128)S(1)} %fusion.38), channel_id=2, replica_groups=mesh['seq'=8,'expert'=4] {'seq'}, use_global_device_ids=true, to_apply=%region_5.7.clone | all-reduce | flops 131072 | bytes 786432
  303.1 0.6 fusion.39
  (45 shorter events, 3.5 us)
Async XLA Ops:
  6.5 36.0 %copy-start = (bf16[1,4,4096]{2,1,0:T(4,128)(2,1)S(1)}, bf16[1,4,4096]{2,1,0:T(4,128)(2,1)}, u32[]{:S(2)}) copy-start(bf16[1,4,4096]{2,1,0:T(4,128)(2,1)} %param.9) | copy-start | bytes 98308
  6.5 115.4 %all-gather.5.cloned.1.call-start = ((), (), s32[]{:S(2)}) async-start(), calls=%async_computation.5 | async-start | bytes 4718592 | tf_op jit(solution)/shard_map/all_gather | solution.py:73
  58.5 25.9 %copy-start.1 = (bf16[1,4,8]{2,1,0:T(4,128)(2,1)S(1)}, bf16[1,4,8]{2,1,0:T(4,128)(2,1)}, u32[]{:S(2)}) copy-start(bf16[1,4,8]{2,1,0:T(4,128)(2,1)} %param.12) | copy-start | bytes 196
  72.9 93.1 %all-gather.3.cloned.1.call-start = ((), (), s32[]{:S(2)}) async-start(), calls=%async_computation.4 | async-start | bytes 4718592 | tf_op jit(solution)/shard_map/all_gather | solution.py:74
  207.4 5.0 %copy-start.2 = (u32[32]{0:T(128)S(1)}, u32[32]{0:T(128)}, u32[]{:S(2)}) copy-start(u32[32]{0:T(128)} %constant.65) | copy-start | bytes 388
  207.4 53.1 %all-to-all-start.3 = ((bf16[4,8,4,4,4096]{4,3,1,0,2:T(4,128)(2,1)}), bf16[4,8,4,4,4096]{4,3,1,0,2:T(4,128)(2,1)}, u32[]{:S(2)}, u32[]{:S(2)}) async-start(bf16[4,8,4,4,4096]{4,3,1,0,2:T(4,128)(2,1)} %copy.41), calls=%async_computation.3 | async-start | bytes 8388608 | tf_op jit(solution)/shard_map/all_to_all | solution.py:83
Sparse Core Ops, SparseCore 0:
  73.1 45.5 all-gather.4
  120.3 45.7 all-gather.2
where the time goes:
time: 311 us
  blocking collectives  134 us (43%)
  waiting for transfers between devices  85.1 us (27%)
  matrix products  35.2 us (11%)
  local copies, waits for them, and re-layouts  34.2 us (11%)
  between operations  14.3 us (5%)
  starting transfers between devices  5.03 us (2%)
    all_to_all x1, waiting for transfers between devices, per_device(): lax.all_to_all(reshaped, 'expert', split_axis=2, concat_axis=0, tiled=True)  46.8 us
    all_gather x1, waiting for transfers between devices, per_device(): lax.all_gather(arrived_dy, 'seq', axis=2, tiled=True)  38.2 us
    unnamed x1, blocking collectives  32.7 us
    reshape x2, local copies, waits for them, and re-layouts, per_device(): part_rows.reshape(local_experts, seq_size, expert_peers, capacity // seq_...  15.1 us
    all_gather x1, blocking collectives, per_device(): lax.all_gather(out_grad, 'seq', axis=1, tiled=True)  14.9 us
    all_gather x1, blocking collectives, per_device(): lax.all_gather(expert_ids, 'seq', axis=1, tiled=True)  14.7 us
    all_gather x1, blocking collectives, per_device(): lax.all_gather(tokens, 'seq', axis=1, tiled=True)  14.7 us
    all_gather x1, blocking collectives, per_device(): lax.all_gather(arrived_gate, 'seq', axis=2, tiled=True)  14.3 us
  transfers between devices with their start and end apart: 3, of which 2 were waited for; matrix products, arithmetic and copies ran while one was open for 3% of the time, Pallas kernels for 0%

commit v1 on v0

--- a/solution.py
+++ b/solution.py
@@ -2,6 +2,12 @@
 import jax.numpy as jnp
 from jax import lax
 from jax.sharding import PartitionSpec as P
+
+
+def tiled_gather(x, axis, dim):
+    size = lax.axis_size(axis)
+    repeats = [size if d == dim else 1 for d in range(x.ndim)]
+    return lax.all_to_all(jnp.tile(x, repeats), axis, split_axis=dim, concat_axis=dim, tiled=True)
 
 
 def swiglu_back(gate_act, up_act, hidden_grad):
@@ -28,7 +34,7 @@
     gathered_x, gathered_dy, gathered_ids, gathered_gates = (
         lax.all_gather(tokens, "seq", axis=1, tiled=True),
         lax.all_gather(out_grad, "seq", axis=1, tiled=True),
-        lax.all_gather(expert_ids, "seq", axis=1, tiled=True),
+        tiled_gather(expert_ids, "seq", 1),
         lax.all_gather(route_gates, "seq", axis=1, tiled=True),
     )
     group_x = gathered_x[0]

time: 311 us -> 307 us (0.987)
  blocking collectives: 134 us -> 120 us
  starting transfers between devices: 5.03 us -> 11.4 us
    all_gather x1 -> x0, blocking collectives: 14.7 us -> none  [per_device(): lax.all_gather(expert_ids, 'seq', axis=1, tiled=True)]
    all_to_all x0 -> x1, starting transfers between devices: none -> 6.35 us  [tiled_gather(): lax.all_to_all(jnp.tile(x, repeats), axis, split_axis=dim, concat_axis=di...]
  transfers between devices with their start and end apart: 3 -> 4, of which waited for: 2 -> 2; matrix products, arithmetic and copies ran while one was open for 3% -> 4% of each run, Pallas kernels for 0% -> 0%
where the time goes in v1:
time: 307 us; the launch traced here: 306 us
  blocking collectives  120 us (39%)
  waiting for transfers between devices  86.7 us (28%)
  local copies, waits for them, and re-layouts  36.3 us (12%)
  matrix products  35.1 us (11%)
  between operations  14.3 us (5%)
  starting transfers between devices  11.4 us (4%)
    all_to_all x1, waiting for transfers between devices, per_device(): lax.all_to_all(reshaped, 'expert', split_axis=2, concat_axis=0, tiled=True)  46.8 us
    all_gather x1, waiting for transfers between devices, per_device(): lax.all_gather(arrived_dy, 'seq', axis=2, tiled=True)  39.8 us
    unnamed x1, blocking collectives  32.7 us
    all_gather x1, blocking collectives, per_device(): lax.all_gather(out_grad, 'seq', axis=1, tiled=True)  15.2 us
    reshape x2, local copies, waits for them, and re-layouts, per_device(): part_rows.reshape(local_experts, seq_size, expert_peers, capacity // seq_...  15.1 us
    all_gather x1, blocking collectives, per_device(): lax.all_gather(tokens, 'seq', axis=1, tiled=True)  14.8 us
    all_gather x1, blocking collectives, per_device(): lax.all_gather(arrived_gate, 'seq', axis=2, tiled=True)  14.6 us
    all_gather x1, blocking collectives, per_device(): lax.all_gather(route_gates, 'seq', axis=1, tiled=True)  13.4 us
  transfers between devices with their start and end apart: 4, of which 2 were waited for; matrix products, arithmetic and copies ran while one was open for 4% of the time, Pallas kernels for 0%

profile of v1, /device:TPU:0, one launch (start us, length us, event | category | flops | bytes accessed | tf_op | source)
XLA Modules:
  0.0 306.3 jit_solution(13285103180171934944)
XLA Ops:
  6.5 1.3 tile.12
  7.8 6.4 %all-to-all-start = ((s32[1,32,8]{2,0,1:T(1,128)}), s32[1,32,8]{2,0,1:T(1,128)S(1)}, u32[]{:S(2)}, u32[]{:S(2)}) async-start(s32[1,32,8]{2,0,1:T(1,128)} %bitcast.1), calls=%async_computation | async-start | bytes 32768 | tf_op jit(solution)/shard_map/all_to_all | solution.py:10
  14.2 0.8 copy.31
  15.0 15.2 %all_gather.18 = bf16[1,32,4096]{2,0,1:T(2,128)(2,1)S(1)} all-gather(bf16[1,4,4096]{2,0,1:T(2,128)(2,1)S(1)} %copy.31), channel_id=1, replica_groups=mesh['seq'=8,'expert'=4] {'seq'}, dimensions={1}, use_global_device_ids=true | all-gather | bytes 294912 | tf_op jit(solution)/shard_map/all_gather | solution.py:36
  30.2 0.8 copy.37
  31.0 14.8 %all_gather.22 = bf16[1,32,4096]{2,0,1:T(2,128)(2,1)S(1)} all-gather(bf16[1,4,4096]{2,0,1:T(2,128)(2,1)S(1)} %copy.37), channel_id=1, replica_groups=mesh['seq'=8,'expert'=4] {'seq'}, dimensions={1}, use_global_device_ids=true | all-gather | bytes 294912 | tf_op jit(solution)/shard_map/all_gather | solution.py:35
  46.6 0.6 reduce-window.6
  47.9 0.7 fusion.50
  48.9 1.4 scatter_custom_fusion
  50.6 0.9 gather_fusion
  51.7 0.9 gather_fusion.1
  53.3 12.5 %all_to_all.74 = bf16[4,4,4,4096]{3,2,1,0:T(4,128)(2,1)S(1)} all-to-all(bf16[4,4,4,4096]{3,2,1,0:T(4,128)(2,1)S(1)} %get-tuple-element.10), channel_id=1, replica_groups=mesh['seq'=8,'expert'=4] {'expert'}, dimensions={0} | all-to-all | bytes 1048576 | tf_op jit(solution)/shard_map/all_to_all | solution.py:74
  66.1 0.9 all_to_all.65
  67.1 10.2 %all_to_all.75 = bf16[4,4,4,4096]{3,2,1,0:T(4,128)(2,1)S(1)} all-to-all(bf16[4,4,4,4096]{3,2,1,0:T(4,128)(2,1)S(1)} %get-tuple-element.11), channel_id=1, replica_groups=mesh['seq'=8,'expert'=4] {'expert'}, dimensions={0} | all-to-all | bytes 1048576 | tf_op jit(solution)/shard_map/all_to_all | solution.py:75
  77.5 0.9 all_to_all.57
  78.5 13.4 %all_gather.20 = bf16[1,32,8]{2,0,1:T(2,128)(2,1)S(1)} all-gather(bf16[1,4,8]{2,0,1:T(2,128)(2,1)S(1)} %copy.33), channel_id=1, replica_groups=mesh['seq'=8,'expert'=4] {'seq'}, dimensions={1}, use_global_device_ids=true | all-gather | bytes 576 | tf_op jit(solution)/shard_map/all_gather | solution.py:38
  92.0 2.2 scatter_custom_fusion.1
  94.4 7.0 %all_to_all.76 = bf16[4,4,4]{2,1,0:T(4,128)(2,1)S(1)} all-to-all(bf16[4,4,4]{2,1,0:T(4,128)(2,1)S(1)} %constant_dynamic-slice_fusion), channel_id=1, replica_groups=mesh['seq'=8,'expert'=4] {'expert'}, dimensions={0} | all-to-all | bytes 256 | tf_op jit(solution)/shard_map/all_to_all | solution.py:76
  101.5 14.6 %all_gather.21 = bf16[1,4,128]{1,0,2:T(2,128)(2,1)S(1)} all-gather(bf16[1,4,16]{1,0,2:T(2,128)(2,1)S(1)} %reshape.132), channel_id=1, replica_groups=mesh['seq'=8,'expert'=4] {'seq'}, dimensions={2}, use_global_device_ids=true | all-gather | bytes 1152 | tf_op jit(solution)/shard_map/all_gather | solution.py:81
  116.2 5.9 %fusion.9 = f32[4,192,128]{2,1,0:T(8,128)S(1)} fusion(bf16[4,192,4096]{2,1,0:T(8,128)(2,1)} %param.13, bf16[1,4,128,4096]{3,2,1,0:T(8,128)(2,1)} %all-gather.5.cloned.1.call-done), kind=kOutput, calls=%fused_computation.12 | convolution fusion | flops 805306368 | bytes 10878976 | tf_op jit(solution)/shard_map/ird,ifd->ifr/dot_general | solution.py:23
  122.1 39.8 %all-gather.3.cloned.1.call-done = bf16[1,4,128,4096]{3,2,1,0:T(8,128)(2,1)} async-done(((bf16[1,4,16,4096]{3,2,1,0:T(8,128)(2,1)}), bf16[1,4,128,4096]{3,2,1,0:T(8,128)(2,1)}) %all-gather.3.cloned.1.call-update) | async-done | bytes 4194320 | tf_op jit(solution)/shard_map/all_gather | solution.py:80
  161.9 5.8 %fusion.24 = f32[4,192,128]{2,1,0:T(8,128)S(1)} fusion(bf16[4,192,4096]{2,1,0:T(8,128)(2,1)} %param.15, bf16[1,4,128,4096]{3,2,1,0:T(8,128)(2,1)} %all-gather.3.cloned.1.call-done, f32[4,128]{1,0:T(4,128)S(1)} %copy.36), kind=kOutput, calls=%fused_computation.17 | convolution fusion | flops 805404672 | bytes 10881024 | tf_op jit(solution)/shard_map/ird,ifd->ifr/dot_general | solution.py:25
  167.7 11.9 %fusion.31 = f32[4,128,4096]{2,1,0:T(8,128)} fusion(bf16[4,192,4096]{2,1,0:T(8,128)(2,1)} %param.13, f32[4,192,128]{2,1,0:T(8,128)S(1)} %fusion.24, bf16[4,192,4096]{2,1,0:T(8,128)(2,1)} %param.14, bf16[1,4,128,4096]{3,2,1,0:T(8,128)(2,1)} %all-gather.5.cloned.1.call-done, f32[4,192,128]{2,1,0:T(8,128)S(1)} %fusion.9), kind=kOutput, calls=%fused_computation.19 | convolution fusion | flops 1611595776 | bytes 25952256 | tf_op jit(solution)/shard_map/ifr,ifd->ird/dot_general | solution.py:28
  179.6 8.5 %add_convert_fusion = bf16[4,128,4096]{2,1,0:T(8,128)(2,1)} fusion(f32[4,128,4096]{2,1,0:T(8,128)} %fusion.31, bf16[4,192,4096]{2,1,0:T(8,128)(2,1)} %param.14, f32[4,192,128]{2,1,0:T(8,128)S(1)} %fusion.24, f32[4,192,128]{2,1,0:T(8,128)S(1)} %fusion.9), kind=kOutput, calls=%fused_computation.4 | convolution fusion | flops 810090496 | bytes 19660800 | tf_op jit(solution)/shard_map/ifr,ifd->ird/dot_general | solution.py:29
  188.2 7.2 %reshape.85 = bf16[4,8,4,4,4096]{4,3,2,1,0:T(4,128)(2,1)} reshape(bf16[4,128,4096]{2,1,0:T(8,128)(2,1)} %add_convert_fusion) | data formatting | bytes 8388608 | tf_op jit(solution)/shard_map/reshape | solution.py:86
  195.4 7.9 %copy.39 = bf16[4,8,4,4,4096]{4,3,1,0,2:T(4,128)(2,1)} copy(bf16[4,8,4,4,4096]{4,3,2,1,0:T(4,128)(2,1)} %reshape.85) | data formatting | bytes 8388608 | tf_op jit(solution)/shard_map/reshape | solution.py:86
  203.2 5.0 %all-to-all-start.4 = ((bf16[4,8,4,4,4096]{4,3,1,0,2:T(4,128)(2,1)}), bf16[4,8,4,4,4096]{4,3,1,0,2:T(4,128)(2,1)}, u32[]{:S(2)}, u32[]{:S(2)}) async-start(bf16[4,8,4,4,4096]{4,3,1,0,2:T(4,128)(2,1)} %copy.39), calls=%async_computation.4 | async-start | bytes 8388608 | tf_op jit(solution)/shard_map/all_to_all | solution.py:89
  209.5 46.8 %all-to-all-done.4 = bf16[4,8,4,4,4096]{4,3,1,0,2:T(4,128)(2,1)} async-done(((bf16[4,8,4,4,4096]{4,3,1,0,2:T(4,128)(2,1)}), bf16[4,8,4,4,4096]{4,3,1,0,2:T(4,128)(2,1)}, u32[]{:S(2)}, u32[]{:S(2)}) %all-to-all-start.4) | async-done | bytes 4194336 | tf_op jit(solution)/shard_map/all_to_all | solution.py:89
  256.3 6.9 %reshape.86 = bf16[512,4096]{1,0:T(8,128)(2,1)} reshape(bf16[4,4,8,1,4,4096]{5,4,2,1,0,3:T(4,128)(2,1)} %bitcast.18) | data formatting | bytes 8388608 | tf_op jit(solution)/shard_map/reshape | solution.py:90
  263.2 3.0 fusion.38
  266.2 32.7 %all-reduce.4 = bf16[32,4096]{1,0:T(8,128)(2,1)S(1)} all-reduce(f32[32,4096]{1,0:T(8,128)S(1)} %fusion.38), channel_id=2, replica_groups=mesh['seq'=8,'expert'=4] {'seq'}, use_global_device_ids=true, to_apply=%region_5.7.clone | all-reduce | flops 131072 | bytes 786432
  298.9 0.6 fusion.39
  (45 shorter events, 4.6 us)
Async XLA Ops:
  7.8 38.7 %all-to-all-start = ((s32[1,32,8]{2,0,1:T(1,128)}), s32[1,32,8]{2,0,1:T(1,128)S(1)}, u32[]{:S(2)}, u32[]{:S(2)}) async-start(s32[1,32,8]{2,0,1:T(1,128)} %bitcast.1), calls=%async_computation | async-start | bytes 32768 | tf_op jit(solution)/shard_map/all_to_all | solution.py:10
  14.2 102.0 %all-gather.5.cloned.1.call-start = ((), (), s32[]{:S(2)}) async-start(), calls=%async_computation.6 | async-start | bytes 4718592 | tf_op jit(solution)/shard_map/all_gather | solution.py:79
  52.6 25.9 %copy-start = (bf16[1,4,8]{2,1,0:T(4,128)(2,1)S(1)}, bf16[1,4,8]{2,1,0:T(4,128)(2,1)}, u32[]{:S(2)}) copy-start(bf16[1,4,8]{2,1,0:T(4,128)(2,1)} %param.12) | copy-start | bytes 196
  67.0 94.8 %all-gather.3.cloned.1.call-start = ((), (), s32[]{:S(2)}) async-start(), calls=%async_computation.5 | async-start | bytes 4718592 | tf_op jit(solution)/shard_map/all_gather | solution.py:80
  203.2 5.0 %copy-start.1 = (u32[32]{0:T(128)S(1)}, u32[32]{0:T(128)}, u32[]{:S(2)}) copy-start(u32[32]{0:T(128)} %constant.65) | copy-start | bytes 388
  203.2 53.1 %all-to-all-start.4 = ((bf16[4,8,4,4,4096]{4,3,1,0,2:T(4,128)(2,1)}), bf16[4,8,4,4,4096]{4,3,1,0,2:T(4,128)(2,1)}, u32[]{:S(2)}, u32[]{:S(2)}) async-start(bf16[4,8,4,4,4096]{4,3,1,0,2:T(4,128)(2,1)} %copy.39), calls=%async_computation.4 | async-start | bytes 8388608 | tf_op jit(solution)/shard_map/all_to_all | solution.py:89
Sparse Core Ops, SparseCore 0:
  67.2 47.1 all-gather.4
  116.0 45.8 all-gather.2
